TPU v7x, 32 devices: a whole 2x2x4 slice. The times are simulated.
32 devices in a mesh: lat: 4 (over y, x), lon: 8 (over z, core).
Axes of the slice: x: 2, y: 2, z: 4, core: 2. Of those that a mesh axis runs over, the one named last changes fastest.
Arguments:
- wind_u: float32 [32, 32, 1024], P(None, 'lat', 'lon'), may hold values from -6 to 6
- wind_v: float32 [32, 32, 1024], P(None, 'lat', 'lon'), may hold values from -6 to 6
Outputs:
- modes: float32 [32, 2, 32, 1024], P(None, None, 'lat', 'lon')
- factor: float32 [32, 32], replicated
All inputs are finite; a program needn't handle non-finite values.
Results may differ from a plain program's by a relative error of at most 0.0003.
Values sent between devices are 32-bit elements; how exact they have to be, the bound alone decides.
A program may use at most 64 MiB of HBM per device.

v0:
```python
import functools
import math

import jax
import jax.numpy as jnp
from jax import lax
from jax.experimental import pallas as pl
from jax.experimental.pallas import tpu as pltpu
from jax.sharding import PartitionSpec as P

MESH = pl.DeviceIdType.MESH
LANES = 128
SUBS = 8
BLOCK = 8
VMEM_BYTES = 8 * 1024 * 1024


def iota(shape, dim):
    return lax.broadcasted_iota(jnp.int32, shape, dim)


def dot(left, right, dims):
    return lax.dot_general(
        left,
        right,
        (dims, ((), ())),
        precision=lax.Precision.HIGHEST,
        preferred_element_type=jnp.float32,
    )


def two(tile):
    high = tile.astype(jnp.bfloat16)
    return high, (tile - high.astype(jnp.float32)).astype(jnp.bfloat16)


def pair_dot(left, right, dims):
    a, b = two(left)
    x, y = two(right)

    def one(m, n):
        return lax.dot_general(m, n, (dims, ((), ())), preferred_element_type=jnp.float32)

    return one(a, x) + (one(a, y) + one(b, x))


def roll(tile, shift):
    shift = shift % LANES
    return tile if shift == 0 else pltpu.roll(tile, shift, 1)


def spread(tile):
    return jnp.broadcast_to(tile, (SUBS, LANES))


def pack_gram(gram):
    n = gram.shape[0]
    return jnp.concatenate([gram[g * SUBS : (g + 1) * SUBS] for g in range(n // SUBS)], axis=1)


def factorize(packed, n):
    groups = n // SUBS
    lane = iota((SUBS, LANES), 1)
    sub = iota((SUBS, LANES), 0)
    rows = []
    for g in range(groups):
        unit = jnp.where(lane == sub + g * SUBS, 1.0, 0.0)
        rows.append(jnp.where(lane < n, unit, roll(packed, n - g * n)))
    pivots = [None] * groups
    for start in range(0, n, BLOCK):
        r = start // SUBS
        columns = [
            [spread(rows[g][:, n + k : n + k + 1]) if g >= r else None for g in range(groups)]
            for k in range(start, start + BLOCK)
        ]
        for step in range(BLOCK):
            k = start + step
            s = k % SUBS
            pivot = spread(columns[step][r][s : s + 1, :])
            pivots[r] = pivot if s == 0 else jnp.where(sub == s, pivot, pivots[r])
            inverse = 1.0 / pivot
            pivot_row = spread(rows[r][s : s + 1, :]) * inverse
            heads = [
                spread(columns[later][r][s : s + 1, :]) * inverse for later in range(step + 1, BLOCK)
            ]
            for g in range(r, groups):
                factor = columns[step][g]
                if g == r:
                    if s == SUBS - 1:
                        continue
                    factor = jnp.where(sub > s, factor, 0.0)
                rows[g] = rows[g] - factor * pivot_row
                for later in range(step + 1, BLOCK):
                    columns[later][g] = columns[later][g] - factor * heads[later - step - 1]
    out = []
    for g in range(groups):
        scaled = rows[g] * (1.0 / jnp.sqrt(pivots[g]))
        keep = (lane < n) | (lane - n >= sub + g * SUBS)
        out.append(jnp.where(keep, scaled, 0.0))
    return jnp.concatenate(out, axis=0)


def kernel(
    sizes,
    u_hbm,
    v_hbm,
    solved_ref,
    first_ref,
    second_ref,
    wind_ref,
    x_ref,
    lat_out,
    lat_in,
    lon_out,
    lon_in,
    pair_buf,
    chip_buf,
    lat_send,
    lat_recv,
    lon_send,
    lon_recv,
    pair_send,
    pair_recv,
    chip_send,
    chip_recv,
    relay_sem,
    local_sem,
):
    lat_size, lon_size, cores = sizes
    _, snaps, cells, width = wind_ref.shape
    depth = lon_size // cores
    chips = lat_size * depth
    lat = lax.axis_index("lat")
    lon = lax.axis_index("lon")
    z = lon // cores
    core = lon % cores
    mine = lat * depth + z
    lat_up = (lat + 1) % lat_size
    lat_down = (lat + lat_size - 1) % lat_size
    east = (lon + 1) % lon_size
    west = (lon + lon_size - 1) % lon_size

    def twin(d):
        other = (core + d) % cores
        return other, (lat, z * cores + other)

    def chip(d):
        other = (mine + d) % chips
        return other, (other // depth, (other % depth) * cores + core)

    barrier = pltpu.get_barrier_semaphore()
    def along(d):
        return [(lat, (z + depth + s) % depth * cores + core) for s in (d, -d)]

    strides = relay_strides(depth)
    peers = [
        ((lat + a) % lat_size, z * cores + (core + b) % cores)
        for a in range(lat_size)
        for b in range(cores)
        if a or b
    ]
    peers += [(lat, east), (lat, west)] + (along(1) if depth > 1 else [])
    for peer in peers:
        pl.semaphore_signal(barrier, inc=1, device_id=peer, device_id_type=MESH)

    loads = [
        pltpu.make_async_copy(hbm, wind_ref.at[f], local_sem.at[f])
        for f, hbm in enumerate((u_hbm, v_hbm))
    ]
    for load in loads:
        load.start()
    for load in loads:
        load.wait()

    lane = iota((SUBS, LANES), 1)
    parts = snaps // SUBS
    winds = [[wind_ref[f, :, i, :] for i in range(cells)] for f in range(2)]
    for f in range(2):
        lat_out[0, f] = winds[f][cells - 1]
        lat_out[1, f] = winds[f][0]
    edge = jnp.zeros((SUBS, LANES), jnp.float32)
    for f in range(2):
        for i in range(cells):
            for t in range(parts):
                q = (f * cells + i) * parts + t
                tile = winds[f][i][t * SUBS : (t + 1) * SUBS]
                edge = jnp.where(lane // 2 == q, roll(tile, 2 * q + 1), edge)
    lon_out[...] = edge

    pl.semaphore_wait(barrier, len(peers))

    copies = []
    for way, target in ((0, lat_up), (1, lat_down)):
        copies.append(
            pltpu.make_async_remote_copy(
                src_ref=lat_out.at[way],
                dst_ref=lat_in.at[way],
                send_sem=lat_send.at[way],
                recv_sem=lat_recv.at[way],
                device_id=(target, lon),
                device_id_type=MESH,
            )
        )
    for way, target in ((0, east), (1, west)):
        copies.append(
            pltpu.make_async_remote_copy(
                src_ref=lon_out,
                dst_ref=lon_in.at[way],
                send_sem=lon_send.at[way],
                recv_sem=lon_recv.at[way],
                device_id=(lat, target),
                device_id_type=MESH,
            )
        )
    for at, copy in enumerate(copies):
        if at == 0:
            pl.when(lat < lat_size - 1)(copy.start)
        elif at == 1:
            pl.when(lat > 0)(copy.start)
        else:
            copy.start()

    def relay(at):
        for peer in along(strides[at]):
            pl.semaphore_signal(relay_sem.at[at], inc=1, device_id=peer, device_id_type=MESH)

    if strides:
        relay(0)

    nlat = lat_size * cells
    step = 2.0 * math.pi / (lon_size * width)
    row_index = lat * cells - 1 + iota((2 * SUBS, LANES), 0)
    cosines = jnp.cos((row_index.astype(jnp.float32) + 0.5 - nlat / 2) * step)
    weights = jnp.where((row_index >= 0) & (row_index < nlat), cosines, 0.0)
    scales = 0.5 / jnp.sqrt(cosines)

    def weight(i):
        return weights[i + 1 : i + 2, :]

    def scale(i):
        return scales[i + 1 : i + 2, :]

    wide = iota((snaps, LANES), 1)

    def lon_inner(tile):
        right = jnp.where(wide == LANES - 1, 0.0, pltpu.roll(tile, LANES - 1, 1))
        return right - jnp.where(wide == 0, 0.0, pltpu.roll(tile, 1, 1))

    def lat_inner(f, i):
        high = weight(i + 1) * winds[f][i + 1] if i + 1 < cells else 0.0
        low = weight(i - 1) * winds[f][i - 1] if i > 0 else 0.0
        return high - low

    for i in range(cells):
        x_ref[i] = lon_inner(winds[1][i]) - lat_inner(0, i)
        x_ref[cells + i] = lon_inner(winds[0][i]) + lat_inner(1, i)

    for at in range(1, len(strides)):
        pl.semaphore_wait(relay_sem.at[at - 1], 2)
        relay(at)

    for at, copy in enumerate(copies):
        if at == 0:
            pl.when(lat > 0)(copy.wait_recv)
        elif at == 1:
            pl.when(lat < lat_size - 1)(copy.wait_recv)
        else:
            copy.wait_recv()

    ends = jnp.where(lane % 2 == 1, roll(lon_in[0], 1), roll(lon_in[1], LANES - 1))
    sign = jnp.where(lane == LANES - 1, 1.0, jnp.where(lane == 0, -1.0, 0.0))

    def lon_edge(f, i):
        pieces = []
        for t in range(parts):
            q = (f * cells + i) * parts + t
            pieces.append(sign * roll(ends, -(2 * q + 1)))
        return jnp.concatenate(pieces, axis=0)

    def lat_edge(f, i):
        total = 0.0
        if i == cells - 1:
            total = total + weight(cells) * lat_in[1, f]
        if i == 0:
            total = total - weight(-1) * lat_in[0, f]
        return total

    columns = []
    for i in range(cells):
        columns.append((x_ref[i] + lon_edge(1, i) - lat_edge(0, i)) * scale(i))
    for i in range(cells):
        columns.append((x_ref[cells + i] + lon_edge(0, i) + lat_edge(1, i)) * scale(i))
    block = jnp.concatenate(columns, axis=1)

    pending = []

    def exchange(buf, slot, count, peer_of, send, recv, at, value):
        buf[at, slot] = value
        for d in range(1, count):
            other, peer = peer_of(d)
            copy = pltpu.make_async_remote_copy(
                src_ref=buf.at[at, slot],
                dst_ref=buf.at[at, slot],
                send_sem=send.at[at, d - 1],
                recv_sem=recv.at[at, slot],
                device_id=peer,
                device_id_type=MESH,
            )
            copy.start()
            pending.append(copy)
        for d in range(1, count):
            other, peer = peer_of(d)
            pltpu.make_async_remote_copy(
                src_ref=buf.at[at, other],
                dst_ref=buf.at[at, other],
                send_sem=send.at[at, d - 1],
                recv_sem=recv.at[at, other],
                device_id=peer,
                device_id_type=MESH,
            ).wait_recv()
        total = buf[at, 0]
        for index in range(1, count):
            total = total + buf[at, index]
        return total

    def merged(value, at):
        value = exchange(pair_buf, core, cores, twin, pair_send, pair_recv, at, value)
        if at == 0 and strides:
            pl.semaphore_wait(relay_sem.at[len(strides) - 1], 2)
        return exchange(chip_buf, mine, chips, chip, chip_send, chip_recv, at, value)

    gram = dot(block, block, ((1,), (1,)))
    first = factorize(merged(pack_gram(gram), 0), snaps)
    solved = dot(first[:, :snaps], block, ((1,), (0,)))
    gram = pair_dot(solved, solved, ((1,), (1,)))
    solved_ref[...] = solved
    first_ref[...] = first
    second_ref[...] = factorize(merged(pack_gram(gram), 1), snaps)

    for at, copy in enumerate(copies + pending):
        if at == 0:
            pl.when(lat < lat_size - 1)(copy.wait_send)
        elif at == 1:
            pl.when(lat > 0)(copy.wait_send)
        else:
            copy.wait_send()


def finish(root, solved_ref, first_ref, second_ref, modes_ref, factor_ref):
    snaps, _, cells, width = modes_ref.shape
    first, second = first_ref[...], second_ref[...]
    modes = pair_dot(second[:, :snaps] * root, solved_ref[...], ((1,), (0,)))
    for f in range(2):
        for i in range(cells):
            at = (f * cells + i) * width
            modes_ref[:, f, i, :] = modes[:, at : at + width]
    upper = [pltpu.roll(m, LANES - snaps, 1)[:, :snaps] for m in (second, first)]
    factor_ref[...] = dot(upper[0], upper[1], ((1,), (0,))) / root


def relay_strides(depth):
    strides, reach = [], 0
    while reach < depth // 2:
        strides.append(max(reach, 1))
        reach += strides[-1]
    return strides


def shards(sizes, wind_u, wind_v):
    snaps, cells, width = wind_u.shape
    lat_size, lon_size, cores = sizes
    chips = lat_size * lon_size // cores
    f32 = jnp.float32
    dma = pltpu.SemaphoreType.DMA
    vmem = pl.BlockSpec(memory_space=pltpu.VMEM)
    hbm = pl.BlockSpec(memory_space=pltpu.HBM)
    held = pl.pallas_call(
        functools.partial(kernel, sizes),
        out_shape=(
            pltpu.VMEM((snaps, 2 * cells * width), f32),
            pltpu.VMEM((snaps, LANES), f32),
            pltpu.VMEM((snaps, LANES), f32),
        ),
        in_specs=[hbm, hbm],
        out_specs=(vmem, vmem, vmem),
        scratch_shapes=[
            pltpu.VMEM((2, snaps, cells, width), f32),
            pltpu.VMEM((2 * cells, snaps, width), f32),
            pltpu.VMEM((2, 2, snaps, width), f32),
            pltpu.VMEM((2, 2, snaps, width), f32),
            pltpu.VMEM((SUBS, LANES), f32),
            pltpu.VMEM((2, SUBS, LANES), f32),
            pltpu.VMEM((2, cores, SUBS, LANES), f32),
            pltpu.VMEM((2, chips, SUBS, LANES), f32),
            dma((2,)),
            dma((2,)),
            dma((2,)),
            dma((2,)),
            dma((2, cores)),
            dma((2, cores)),
            dma((2, chips)),
            dma((2, chips)),
            pltpu.SemaphoreType.REGULAR((max(len(relay_strides(lon_size // cores)), 1),)),
            dma((2,)),
        ],
        compiler_params=pltpu.CompilerParams(
            collective_id=0, has_side_effects=True, vmem_limit_bytes=VMEM_BYTES
        ),
    )(*(pltpu.with_memory_space_constraint(w, pltpu.HBM) for w in (wind_u, wind_v)))
    root = math.sqrt(2 * lat_size * cells * lon_size * width)
    return pl.pallas_call(
        functools.partial(finish, root),
        out_shape=(
            jax.ShapeDtypeStruct((snaps, 2, cells, width), f32),
            jax.ShapeDtypeStruct((snaps, snaps), f32),
        ),
        in_specs=[vmem, vmem, vmem],
        out_specs=(vmem, vmem),
        compiler_params=pltpu.CompilerParams(vmem_limit_bytes=VMEM_BYTES),
    )(*held)


def solution(mesh):
    lat_size, lon_size = mesh.shape["lat"], mesh.shape["lon"]
    sizes = (lat_size, lon_size, 2 if lon_size % 2 == 0 else 1)
    in_specs = (P(None, "lat", "lon"), P(None, "lat", "lon"))
    out_specs = (P(None, None, "lat", "lon"), P())
    return jax.shard_map(
        functools.partial(shards, sizes),
        mesh=mesh,
        in_specs=in_specs,
        out_specs=out_specs,
        check_vma=False,
    )
```

profile of v0, /device:TPU:0, one launch (start us, length us, event | category | flops | bytes accessed | tf_op | source)
XLA Modules:
  0.0 25.0 jit_solution(17761065395066929980)
XLA Ops:
  0.6 23.3 %shard_map.41 = (f32[32,2048]{1,0:T(8,128)S(1)}, f32[32,128]{1,0:T(8,128)S(1)}, f32[32,128]{1,0:T(8,128)S(1)}) custom-call(f32[32,8,128]{2,1,0:T(8,128)} %u_hbm.1, f32[32,8,128]{2,1,0:T(8,128)} %v_hbm.1), custom_call_target="tpu_custom_call" | custom-call | tf_op jit(solution)/shard_map/pallas_call | solution.py:377
  24.0 1.1 %shard_map.42 = (f32[32,2,8,128]{3,2,1,0:T(8,128)}, f32[32,32]{1,0:T(8,128)}) custom-call(f32[32,2048]{1,0:T(8,128)S(1)} %get-tuple-element.5.solved_ref, f32[32,128]{1,0:T(8,128)S(1)} %get-tuple-element.6.first_ref, f32[32,128]{1,0:T(8,128)S(1)} %get-tuple-element.7.second_ref), custom_call_target="tpu_custom_call" | custom-call | tf_op jit(solution)/shard_map/pallas_call | solution.py:411
where the time goes:
time: 25.2 us; the launch traced here: 25 us
  Pallas kernels  24.4 us (97%)
  between operations  0.64 us (3%)
    pallas_call x1, Pallas kernels, shards(): pl.pallas_call(functools.partial(kernel, sizes), out_shape=(pltpu.VMEM((s...  23.3 us
    pallas_call x1, Pallas kernels, shards(): pl.pallas_call(functools.partial(finish, root), out_shape=(jax.ShapeDtype...  1.06 us

commit v1 on v0

--- a/solution.py
+++ b/solution.py
@@ -53,20 +53,36 @@
     return jnp.broadcast_to(tile, (SUBS, LANES))
 
 
-def pack_gram(gram):
-    n = gram.shape[0]
-    return jnp.concatenate([gram[g * SUBS : (g + 1) * SUBS] for g in range(n // SUBS)], axis=1)
-
-
-def factorize(packed, n):
+def two_sum(a, b):
+    total = a + b
+    part = total - a
+    return total, (a - (total - part)) + (b - part)
+
+
+def power_above(bound):
+    wide = bound * (2.0**23 + 1.0)
+    return 2.0 * jnp.abs(wide - wide * (1.0 - 2.0**-24))
+
+
+def fixed_slices(tile, unit, bits):
+    out = []
+    for count in bits:
+        magic = unit * (1.5 * 2.0 ** (23 - count))
+        part = (tile + magic) - magic
+        out.append(part.astype(jnp.bfloat16))
+        tile = tile - part
+    out.append(tile.astype(jnp.bfloat16))
+    return out
+
+
+def factorize(rows, n):
     groups = n // SUBS
     lane = iota((SUBS, LANES), 1)
     sub = iota((SUBS, LANES), 0)
-    rows = []
-    for g in range(groups):
-        unit = jnp.where(lane == sub + g * SUBS, 1.0, 0.0)
-        rows.append(jnp.where(lane < n, unit, roll(packed, n - g * n)))
+    rows = list(rows)
     pivots = [None] * groups
+    lower = [jnp.zeros((SUBS, LANES), jnp.float32)] * groups
+    across = jnp.ones((SUBS, LANES), jnp.float32)
     for start in range(0, n, BLOCK):
         r = start // SUBS
         columns = [
@@ -78,6 +94,7 @@
             s = k % SUBS
             pivot = spread(columns[step][r][s : s + 1, :])
             pivots[r] = pivot if s == 0 else jnp.where(sub == s, pivot, pivots[r])
+            across = jnp.where(lane == n + k, pivot, across)
             inverse = 1.0 / pivot
             pivot_row = spread(rows[r][s : s + 1, :]) * inverse
             heads = [
@@ -85,6 +102,7 @@
             ]
             for g in range(r, groups):
                 factor = columns[step][g]
+                lower[g] = jnp.where(lane == n + k, factor, lower[g])
                 if g == r:
                     if s == SUBS - 1:
                         continue
@@ -92,21 +110,107 @@
                 rows[g] = rows[g] - factor * pivot_row
                 for later in range(step + 1, BLOCK):
                     columns[later][g] = columns[later][g] - factor * heads[later - step - 1]
-    out = []
+    across = 1.0 / jnp.sqrt(across)
+    out, left = [], []
     for g in range(groups):
         scaled = rows[g] * (1.0 / jnp.sqrt(pivots[g]))
-        keep = (lane < n) | (lane - n >= sub + g * SUBS)
-        out.append(jnp.where(keep, scaled, 0.0))
-    return jnp.concatenate(out, axis=0)
+        at = lane - n - g * SUBS
+        out.append(jnp.where((lane < n) | (at >= sub), scaled, 0.0))
+        left.append(jnp.where((lane >= n) & (at <= sub), lower[g] * across, 0.0))
+    return jnp.concatenate(out, axis=0), jnp.concatenate(left, axis=0)
+
+
+def packed_gram(block, n):
+    groups = n // SUBS
+    peak = jnp.max(jnp.abs(block), axis=1, keepdims=True)
+    unit = power_above(jnp.broadcast_to(peak, (n, LANES)))
+    pieces = []
+    for at in range(0, block.shape[1], LANES):
+        pieces.append(fixed_slices(block[:, at : at + LANES], unit, (5, 12, 19)))
+    stack = jnp.concatenate(
+        [jnp.concatenate([piece[a] for piece in pieces], axis=1) for a in range(4)], axis=0
+    )
+    gram = lax.dot_general(
+        stack, stack, (((1,), (1,)), ((), ())), preferred_element_type=jnp.float32
+    )
+    quarter = iota((SUBS, LANES), 1) // n
+
+    def tile(a, g):
+        at = a * n + g * SUBS
+        return roll(gram[at : at + SUBS], a * n)
+
+    near, far = [], []
+    for g in range(groups):
+        turned = [tile(a, g) for a in range(4)]
+        held = [turned[0]] + [jnp.where(quarter >= a, turned[a], 0.0) for a in range(1, 4)]
+        past = [jnp.where(quarter < a, turned[a], 0.0) for a in range(1, 4)]
+        near.append((held[0] + held[3]) + (held[1] + held[2]))
+        far.append((past[0] + past[2]) + past[1])
+
+    def gather(tiles, order):
+        total = None
+        for g in range(groups):
+            moved = roll(tiles[g], n * (g - order))
+            total = moved if total is None else jnp.where(quarter == g, moved, total)
+        return total
+
+    order = [gather(near, o) for o in range(4)]
+    rest = gather(far, 0) + (gather(far, 1) + gather(far, 2))
+    high, low = two_sum(order[0], order[1])
+    high, more = two_sum(high, order[2])
+    return two_sum(high, (low + more) + (order[3] + rest))
+
+
+def residual(high, low, lower, n):
+    groups = n // SUBS
+    lane = iota((SUBS, LANES), 1)
+    sub = iota((SUBS, LANES), 0)
+    unpacked = [roll(high, -g * n) for g in range(groups)]
+    diagonal = jnp.concatenate(
+        [jnp.where(lane == sub + g * SUBS, unpacked[g], 0.0) for g in range(groups)], axis=0
+    )
+    peak = jnp.sqrt(jnp.sum(diagonal, axis=1, keepdims=True)) * 1.01
+    unit = power_above(jnp.broadcast_to(peak, (n, LANES)))
+    slices = fixed_slices(lower, unit, (8, 17, 26))
+    stack = jnp.concatenate(slices, axis=0)
+    products = [
+        lax.dot_general(
+            stack[:, : 2 * n],
+            one[:, : 2 * n],
+            (((1,), (1,)), ((), ())),
+            preferred_element_type=jnp.float32,
+        )
+        for one in slices
+    ]
+
+    def order(count):
+        total = None
+        for a in range(4):
+            b = count - a
+            if 0 <= b < 4:
+                one = products[b][a * n : (a + 1) * n]
+                total = one if total is None else total + one
+        return total
+
+    def rows_of(packed):
+        return jnp.concatenate(
+            [roll(packed, -g * n)[:, :n] for g in range(groups)], axis=0
+        )
+
+    first, low_one = two_sum(rows_of(high), -order(0))
+    first, low_two = two_sum(first, -order(1))
+    first, low_three = two_sum(first, -order(2))
+    tail = (low_one + low_two) + (low_three + (rows_of(low) - (order(3) + (order(4) + order(5)))))
+    return first + tail
 
 
 def kernel(
     sizes,
+    root,
     u_hbm,
     v_hbm,
-    solved_ref,
-    first_ref,
-    second_ref,
+    modes_ref,
+    factor_ref,
     wind_ref,
     x_ref,
     lat_out,
@@ -294,68 +398,81 @@
 
     pending = []
 
-    def exchange(buf, slot, count, peer_of, send, recv, at, value):
-        buf[at, slot] = value
+    def exchange(buf, slot, count, peer_of, send, recv, pair):
+        for part in range(2):
+            buf[slot, part] = pair[part]
         for d in range(1, count):
             other, peer = peer_of(d)
             copy = pltpu.make_async_remote_copy(
-                src_ref=buf.at[at, slot],
-                dst_ref=buf.at[at, slot],
-                send_sem=send.at[at, d - 1],
-                recv_sem=recv.at[at, slot],
+                src_ref=buf.at[slot],
+                dst_ref=buf.at[slot],
+                send_sem=send,
+                recv_sem=recv,
                 device_id=peer,
                 device_id_type=MESH,
             )
             copy.start()
-            pending.append(copy)
-        for d in range(1, count):
-            other, peer = peer_of(d)
-            pltpu.make_async_remote_copy(
-                src_ref=buf.at[at, other],
-                dst_ref=buf.at[at, other],
-                send_sem=send.at[at, d - 1],
-                recv_sem=recv.at[at, other],
-                device_id=peer,
-                device_id_type=MESH,
-            ).wait_recv()
-        total = buf[at, 0]
-        for index in range(1, count):
-            total = total + buf[at, index]
-        return total
-
-    def merged(value, at):
-        value = exchange(pair_buf, core, cores, twin, pair_send, pair_recv, at, value)
-        if at == 0 and strides:
-            pl.semaphore_wait(relay_sem.at[len(strides) - 1], 2)
-        return exchange(chip_buf, mine, chips, chip, chip_send, chip_recv, at, value)
-
-    gram = dot(block, block, ((1,), (1,)))
-    first = factorize(merged(pack_gram(gram), 0), snaps)
-    solved = dot(first[:, :snaps], block, ((1,), (0,)))
-    gram = pair_dot(solved, solved, ((1,), (1,)))
-    solved_ref[...] = solved
-    first_ref[...] = first
-    second_ref[...] = factorize(merged(pack_gram(gram), 1), snaps)
-
-    for at, copy in enumerate(copies + pending):
+        arrived = buf.at[pl.ds(0, count - 1)]
+        pending.append((arrived, send))
+        pltpu.make_async_copy(arrived, arrived, recv).wait()
+        totals = [(buf[index, 0], buf[index, 1]) for index in range(count)]
+        while len(totals) > 1:
+            merged = []
+            for at in range(0, len(totals) - 1, 2):
+                (a, b), (x, y) = totals[at], totals[at + 1]
+                high, low = two_sum(a, x)
+                merged.append((high, low + (b + y)))
+            if len(totals) % 2:
+                merged.append(totals[-1])
+            totals = merged
+        return two_sum(*totals[0])
+
+    pair = packed_gram(block, snaps)
+    if cores > 1:
+        pair = exchange(pair_buf, core, cores, twin, pair_send, pair_recv, pair)
+    if strides:
+        pl.semaphore_wait(relay_sem.at[len(strides) - 1], 2)
+    if chips > 1:
+        pair = exchange(chip_buf, mine, chips, chip, chip_send, chip_recv, pair)
+    high, low = pair
+
+    groups = snaps // SUBS
+    sub = iota((SUBS, LANES), 0)
+    start = []
+    for g in range(groups):
+        unit = jnp.where(lane == sub + g * SUBS, 1.0, 0.0)
+        start.append(jnp.where(lane < snaps, unit, roll(high, snaps - g * snaps)))
+    first, lower = factorize(start, snaps)
+    inverse = first[:, :snaps]
+    solved = dot(inverse, block, ((1,), (0,)))
+    gap = residual(high, low, lower, snaps)
+    wide_inverse = jnp.concatenate([jnp.zeros_like(inverse), inverse], axis=0)
+    moved = pair_dot(gap, wide_inverse, ((1,), (1,)))
+    moved = pair_dot(
+        inverse, jnp.concatenate([moved, jnp.zeros_like(moved)], axis=1), ((1,), (0,))
+    )
+    start = []
+    for g in range(groups):
+        at = sub + g * SUBS
+        unit = jnp.where((lane == at) | (lane == at + snaps), 1.0, 0.0)
+        start.append(moved[g * SUBS : (g + 1) * SUBS] + unit)
+    second, _ = factorize(start, snaps)
+    modes = pair_dot(second[:, :snaps] * root, solved, ((1,), (0,)))
+    for f in range(2):
+        for i in range(cells):
+            at = (f * cells + i) * width
+            modes_ref[:, f, i, :] = modes[:, at : at + width]
+    factor_ref[...] = dot(second[:, : 2 * snaps], lower[:, : 2 * snaps], ((1,), (1,))) / root
+
+    for at, copy in enumerate(copies):
         if at == 0:
             pl.when(lat < lat_size - 1)(copy.wait_send)
         elif at == 1:
             pl.when(lat > 0)(copy.wait_send)
         else:
             copy.wait_send()
-
-
-def finish(root, solved_ref, first_ref, second_ref, modes_ref, factor_ref):
-    snaps, _, cells, width = modes_ref.shape
-    first, second = first_ref[...], second_ref[...]
-    modes = pair_dot(second[:, :snaps] * root, solved_ref[...], ((1,), (0,)))
-    for f in range(2):
-        for i in range(cells):
-            at = (f * cells + i) * width
-            modes_ref[:, f, i, :] = modes[:, at : at + width]
-    upper = [pltpu.roll(m, LANES - snaps, 1)[:, :snaps] for m in (second, first)]
-    factor_ref[...] = dot(upper[0], upper[1], ((1,), (0,))) / root
+    for sent, send in pending:
+        pltpu.make_async_copy(sent, sent, send).wait()
 
 
 def relay_strides(depth):
@@ -374,15 +491,15 @@
     dma = pltpu.SemaphoreType.DMA
     vmem = pl.BlockSpec(memory_space=pltpu.VMEM)
     hbm = pl.BlockSpec(memory_space=pltpu.HBM)
-    held = pl.pallas_call(
-        functools.partial(kernel, sizes),
+    root = math.sqrt(2 * lat_size * cells * lon_size * width)
+    return pl.pallas_call(
+        functools.partial(kernel, sizes, root),
         out_shape=(
-            pltpu.VMEM((snaps, 2 * cells * width), f32),
-            pltpu.VMEM((snaps, LANES), f32),
-            pltpu.VMEM((snaps, LANES), f32),
+            jax.ShapeDtypeStruct((snaps, 2, cells, width), f32),
+            jax.ShapeDtypeStruct((snaps, snaps), f32),
         ),
         in_specs=[hbm, hbm],
-        out_specs=(vmem, vmem, vmem),
+        out_specs=(vmem, vmem),
         scratch_shapes=[
             pltpu.VMEM((2, snaps, cells, width), f32),
             pltpu.VMEM((2 * cells, snaps, width), f32),
@@ -390,16 +507,16 @@
             pltpu.VMEM((2, 2, snaps, width), f32),
             pltpu.VMEM((SUBS, LANES), f32),
             pltpu.VMEM((2, SUBS, LANES), f32),
-            pltpu.VMEM((2, cores, SUBS, LANES), f32),
-            pltpu.VMEM((2, chips, SUBS, LANES), f32),
+            pltpu.VMEM((cores, 2, SUBS, LANES), f32),
+            pltpu.VMEM((chips, 2, SUBS, LANES), f32),
             dma((2,)),
             dma((2,)),
             dma((2,)),
             dma((2,)),
-            dma((2, cores)),
-            dma((2, cores)),
-            dma((2, chips)),
-            dma((2, chips)),
+            dma,
+            dma,
+            dma,
+            dma,
             pltpu.SemaphoreType.REGULAR((max(len(relay_strides(lon_size // cores)), 1),)),
             dma((2,)),
         ],
@@ -407,17 +524,6 @@
             collective_id=0, has_side_effects=True, vmem_limit_bytes=VMEM_BYTES
         ),
     )(*(pltpu.with_memory_space_constraint(w, pltpu.HBM) for w in (wind_u, wind_v)))
-    root = math.sqrt(2 * lat_size * cells * lon_size * width)
-    return pl.pallas_call(
-        functools.partial(finish, root),
-        out_shape=(
-            jax.ShapeDtypeStruct((snaps, 2, cells, width), f32),
-            jax.ShapeDtypeStruct((snaps, snaps), f32),
-        ),
-        in_specs=[vmem, vmem, vmem],
-        out_specs=(vmem, vmem),
-        compiler_params=pltpu.CompilerParams(vmem_limit_bytes=VMEM_BYTES),
-    )(*held)
 
 
 def solution(mesh):

time: 25.2 us -> 20.5 us (0.81)
  Pallas kernels: 24.4 us -> 18.4 us
  local copies, waits for them, and re-layouts: 0 us -> 1.31 us
    pallas_call x2 -> x1, Pallas kernels: 24.4 us -> 18.4 us  [shards(): pl.pallas_call(functools.partial(kernel, sizes, root), out_shape=(jax.Sha...]
    unnamed x0 -> x2, local copies, waits for them, and re-layouts: none -> 1.31 us
where the time goes in v1:
time: 20.5 us; the launch traced here: 20.4 us
  Pallas kernels  18.4 us (90%)
  local copies, waits for them, and re-layouts  1.31 us (6%)
  between operations  0.64 us (3%)
    pallas_call x1, Pallas kernels, shards(): pl.pallas_call(functools.partial(kernel, sizes, root), out_shape=(jax.Sha...  18.4 us
    unnamed x2, local copies, waits for them, and re-layouts  1.31 us

profile of v1, /device:TPU:0, one launch (start us, length us, event | category | flops | bytes accessed | tf_op | source)
XLA Modules:
  0.0 20.4 jit_solution(10614898638258096318)
XLA Ops:
  0.6 18.4 %shard_map.41 = (f32[32,2,8,128]{3,2,1,0:T(8,128)S(1)}, f32[32,32]{1,0:T(8,128)S(1)}) custom-call(f32[32,8,128]{2,1,0:T(8,128)} %u_hbm.1, f32[32,8,128]{2,1,0:T(8,128)} %v_hbm.1), custom_call_target="tpu_custom_call" | custom-call | tf_op jit(solution)/shard_map/pallas_call | solution.py:495
  19.1 0.7 %copy.6 = f32[32,2,8,128]{3,2,1,0:T(8,128)} copy(f32[32,2,8,128]{3,2,1,0:T(8,128)S(1)} %get-tuple-element.4) | data formatting | bytes 524288
  19.8 0.6 %copy.7 = f32[32,32]{1,0:T(8,128)} copy(f32[32,32]{1,0:T(8,128)S(1)} %get-tuple-element.5) | data formatting | bytes 8192

commit v2 on v1

--- a/solution.py
+++ b/solution.py
@@ -11,7 +11,7 @@
 MESH = pl.DeviceIdType.MESH
 LANES = 128
 SUBS = 8
-BLOCK = 8
+DIRECT = 64
 VMEM_BYTES = 8 * 1024 * 1024
 
 
@@ -75,48 +75,43 @@
     return out
 
 
-def factorize(rows, n):
+def factorize(source, n):
     groups = n // SUBS
     lane = iota((SUBS, LANES), 1)
     sub = iota((SUBS, LANES), 0)
-    rows = list(rows)
+    columns = {
+        (g, k): spread(source(g, k)) for k in range(n) for g in range(k // SUBS, groups)
+    }
+    rows = [jnp.where(lane == sub + g * SUBS, 1.0, 0.0) for g in range(groups)]
     pivots = [None] * groups
     lower = [jnp.zeros((SUBS, LANES), jnp.float32)] * groups
     across = jnp.ones((SUBS, LANES), jnp.float32)
-    for start in range(0, n, BLOCK):
-        r = start // SUBS
-        columns = [
-            [spread(rows[g][:, n + k : n + k + 1]) if g >= r else None for g in range(groups)]
-            for k in range(start, start + BLOCK)
-        ]
-        for step in range(BLOCK):
-            k = start + step
-            s = k % SUBS
-            pivot = spread(columns[step][r][s : s + 1, :])
-            pivots[r] = pivot if s == 0 else jnp.where(sub == s, pivot, pivots[r])
-            across = jnp.where(lane == n + k, pivot, across)
-            inverse = 1.0 / pivot
-            pivot_row = spread(rows[r][s : s + 1, :]) * inverse
-            heads = [
-                spread(columns[later][r][s : s + 1, :]) * inverse for later in range(step + 1, BLOCK)
-            ]
-            for g in range(r, groups):
-                factor = columns[step][g]
-                lower[g] = jnp.where(lane == n + k, factor, lower[g])
-                if g == r:
-                    if s == SUBS - 1:
-                        continue
-                    factor = jnp.where(sub > s, factor, 0.0)
-                rows[g] = rows[g] - factor * pivot_row
-                for later in range(step + 1, BLOCK):
-                    columns[later][g] = columns[later][g] - factor * heads[later - step - 1]
+    for k in range(n):
+        r, s = divmod(k, SUBS)
+        pivot = spread(columns[r, k][s : s + 1, :])
+        pivots[r] = pivot if s == 0 else jnp.where(sub == s, pivot, pivots[r])
+        across = jnp.where(lane == n + k, pivot, across)
+        inverse = 1.0 / pivot
+        scaled = {g: columns[g, k] * inverse for g in range(r, groups)}
+        for j in range(k + 1, n):
+            head = spread(columns[j // SUBS, k][j % SUBS : j % SUBS + 1, :])
+            for g in range(j // SUBS, groups):
+                columns[g, j] = columns[g, j] - scaled[g] * head
+        pivot_row = spread(rows[r][s : s + 1, :])
+        for g in range(r, groups):
+            lower[g] = jnp.where(lane == n + k, columns[g, k], lower[g])
+            factor = scaled[g]
+            if g == r:
+                if s == SUBS - 1:
+                    continue
+                factor = jnp.where(sub > s, factor, 0.0)
+            rows[g] = rows[g] - factor * pivot_row
     across = 1.0 / jnp.sqrt(across)
     out, left = [], []
     for g in range(groups):
-        scaled = rows[g] * (1.0 / jnp.sqrt(pivots[g]))
-        at = lane - n - g * SUBS
-        out.append(jnp.where((lane < n) | (at >= sub), scaled, 0.0))
-        left.append(jnp.where((lane >= n) & (at <= sub), lower[g] * across, 0.0))
+        out.append(rows[g] * (1.0 / jnp.sqrt(pivots[g])))
+        keep = (lane >= n) & (lane - n - g * SUBS <= sub)
+        left.append(jnp.where(keep, lower[g] * across, 0.0))
     return jnp.concatenate(out, axis=0), jnp.concatenate(left, axis=0)
 
 
@@ -158,18 +153,40 @@
     rest = gather(far, 0) + (gather(far, 1) + gather(far, 2))
     high, low = two_sum(order[0], order[1])
     high, more = two_sum(high, order[2])
-    return two_sum(high, (low + more) + (order[3] + rest))
-
-
-def residual(high, low, lower, n):
+    high, low = two_sum(high, (low + more) + (order[3] + rest))
+    ahead = place(n)
+    edge = jnp.sum(jnp.where(ahead == 0, low, 0.0), axis=0, keepdims=True)
+    return jnp.where(ahead > 0, low, high), edge
+
+
+def place(n):
+    lane = iota((SUBS, LANES), 1)
+    return lane % n - (lane // n * SUBS + iota((SUBS, LANES), 0))
+
+
+def residual(total, error, edge, lower, n):
     groups = n // SUBS
-    lane = iota((SUBS, LANES), 1)
-    sub = iota((SUBS, LANES), 0)
-    unpacked = [roll(high, -g * n) for g in range(groups)]
-    diagonal = jnp.concatenate(
-        [jnp.where(lane == sub + g * SUBS, unpacked[g], 0.0) for g in range(groups)], axis=0
-    )
-    peak = jnp.sqrt(jnp.sum(diagonal, axis=1, keepdims=True)) * 1.01
+    shape = (n, n)
+    row, col = iota(shape, 0), iota(shape, 1)
+
+    def unpack(packed):
+        return jnp.concatenate([roll(packed, -g * n) for g in range(groups)], axis=0)
+
+    def flip(tile):
+        return jnp.transpose(tile)[:n]
+
+    whole, rest = unpack(total), unpack(error)
+    whole_flip, rest_flip = flip(whole)[:, :n], flip(rest)[:, :n]
+    whole, rest = whole[:, :n], rest[:, :n]
+    diagonal = jnp.zeros((1, LANES), jnp.float32)
+    lane = iota((1, LANES), 1)
+    for g in range(groups):
+        diagonal = jnp.where(lane // SUBS == g, roll(edge, -g * n), diagonal)
+    diagonal = jnp.broadcast_to(diagonal[:, :n], shape)
+    high = jnp.where(row >= col, whole, whole_flip)
+    low = jnp.where(row > col, rest + whole_flip, rest_flip + whole)
+    low = jnp.where(row == col, rest + diagonal, low)
+    peak = jnp.sqrt(jnp.sum(jnp.where(row == col, high, 0.0), axis=1, keepdims=True)) * 1.01
     unit = power_above(jnp.broadcast_to(peak, (n, LANES)))
     slices = fixed_slices(lower, unit, (8, 17, 26))
     stack = jnp.concatenate(slices, axis=0)
@@ -192,15 +209,10 @@
                 total = one if total is None else total + one
         return total
 
-    def rows_of(packed):
-        return jnp.concatenate(
-            [roll(packed, -g * n)[:, :n] for g in range(groups)], axis=0
-        )
-
-    first, low_one = two_sum(rows_of(high), -order(0))
+    first, low_one = two_sum(high, -order(0))
     first, low_two = two_sum(first, -order(1))
     first, low_three = two_sum(first, -order(2))
-    tail = (low_one + low_two) + (low_three + (rows_of(low) - (order(3) + (order(4) + order(5)))))
+    tail = (low_one + low_two) + (low_three + (low - (order(3) + (order(4) + order(5)))))
     return first + tail
 
 
@@ -209,29 +221,27 @@
     root,
     u_hbm,
     v_hbm,
-    modes_ref,
+    solved_ref,
+    turn_ref,
     factor_ref,
     wind_ref,
     x_ref,
-    lat_out,
+    hold_ref,
     lat_in,
     lon_out,
     lon_in,
-    pair_buf,
-    chip_buf,
+    sum_bufs,
     lat_send,
     lat_recv,
     lon_send,
     lon_recv,
-    pair_send,
-    pair_recv,
-    chip_send,
-    chip_recv,
+    sum_send,
+    sum_recv,
     relay_sem,
     local_sem,
 ):
     lat_size, lon_size, cores = sizes
-    _, snaps, cells, width = wind_ref.shape
+    _, cells, snaps, width = wind_ref.shape
     depth = lon_size // cores
     chips = lat_size * depth
     lat = lax.axis_index("lat")
@@ -244,15 +254,16 @@
     east = (lon + 1) % lon_size
     west = (lon + lon_size - 1) % lon_size
 
-    def twin(d):
-        other = (core + d) % cores
-        return other, (lat, z * cores + other)
-
-    def chip(d):
-        other = (mine + d) % chips
-        return other, (other // depth, (other % depth) * cores + core)
+    loads = [
+        pltpu.make_async_copy(hbm.at[:, i], wind_ref.at[f, i], local_sem)
+        for f, hbm in enumerate((u_hbm, v_hbm))
+        for i in range(cells)
+    ]
+    for load in loads:
+        load.start()
 
     barrier = pltpu.get_barrier_semaphore()
+
     def along(d):
         return [(lat, (z + depth + s) % depth * cores + core) for s in (d, -d)]
 
@@ -267,29 +278,21 @@
     for peer in peers:
         pl.semaphore_signal(barrier, inc=1, device_id=peer, device_id_type=MESH)
 
-    loads = [
-        pltpu.make_async_copy(hbm, wind_ref.at[f], local_sem.at[f])
-        for f, hbm in enumerate((u_hbm, v_hbm))
-    ]
-    for load in loads:
-        load.start()
-    for load in loads:
-        load.wait()
+    pltpu.make_async_copy(wind_ref, wind_ref, local_sem).wait()
 
     lane = iota((SUBS, LANES), 1)
     parts = snaps // SUBS
-    winds = [[wind_ref[f, :, i, :] for i in range(cells)] for f in range(2)]
-    for f in range(2):
-        lat_out[0, f] = winds[f][cells - 1]
-        lat_out[1, f] = winds[f][0]
-    edge = jnp.zeros((SUBS, LANES), jnp.float32)
+    winds = [[wind_ref[f, i] for i in range(cells)] for f in range(2)]
+    edges = [jnp.zeros((SUBS, LANES), jnp.float32)] * parts
     for f in range(2):
         for i in range(cells):
             for t in range(parts):
                 q = (f * cells + i) * parts + t
                 tile = winds[f][i][t * SUBS : (t + 1) * SUBS]
-                edge = jnp.where(lane // 2 == q, roll(tile, 2 * q + 1), edge)
-    lon_out[...] = edge
+                edges[t] = jnp.where(lane // 2 == q, roll(tile, 2 * q + 1), edges[t])
+    while len(edges) > 1:
+        edges = [sum(edges[at : at + 2]) for at in range(0, len(edges), 2)]
+    lon_out[...] = edges[0]
 
     pl.semaphore_wait(barrier, len(peers))
 
@@ -297,7 +300,7 @@
     for way, target in ((0, lat_up), (1, lat_down)):
         copies.append(
             pltpu.make_async_remote_copy(
-                src_ref=lat_out.at[way],
+                src_ref=wind_ref.at[:, 0 if way else cells - 1],
                 dst_ref=lat_in.at[way],
                 send_sem=lat_send.at[way],
                 recv_sem=lat_recv.at[way],
@@ -398,24 +401,32 @@
 
     pending = []
 
-    def exchange(buf, slot, count, peer_of, send, recv, pair):
-        for part in range(2):
-            buf[slot, part] = pair[part]
-        for d in range(1, count):
-            other, peer = peer_of(d)
+    def exchange(buf, slot, count, target, at, parts):
+        rows = 0
+        for part in parts:
+            buf[slot, pl.ds(rows, part.shape[0])] = part
+            rows += part.shape[0]
+        for d in peer_order(count):
             copy = pltpu.make_async_remote_copy(
                 src_ref=buf.at[slot],
                 dst_ref=buf.at[slot],
-                send_sem=send,
-                recv_sem=recv,
-                device_id=peer,
-                device_id_type=MESH,
+                send_sem=sum_send.at[at],
+                recv_sem=sum_recv.at[at],
+                device_id=target(shifted(slot, d, count)),
+                device_id_type=pl.DeviceIdType.LOGICAL,
             )
             copy.start()
         arrived = buf.at[pl.ds(0, count - 1)]
-        pending.append((arrived, send))
-        pltpu.make_async_copy(arrived, arrived, recv).wait()
-        totals = [(buf[index, 0], buf[index, 1]) for index in range(count)]
+        pending.append((arrived, sum_send.at[at]))
+        pltpu.make_async_copy(arrived, arrived, sum_recv.at[at]).wait()
+        edges = [buf[index, pl.ds(SUBS, 1)] for index in range(count)]
+        while len(edges) > 1:
+            edges = [sum(edges[at : at + 2]) for at in range(0, len(edges), 2)]
+        zero = jnp.zeros((SUBS, LANES), jnp.float32)
+        totals = []
+        for index in range(count):
+            error = buf[index, pl.ds(SUBS + 1, SUBS)] if len(parts) > 2 else zero
+            totals.append((buf[index, pl.ds(0, SUBS)], error))
         while len(totals) > 1:
             merged = []
             for at in range(0, len(totals) - 1, 2):
@@ -425,44 +436,39 @@
             if len(totals) % 2:
                 merged.append(totals[-1])
             totals = merged
-        return two_sum(*totals[0])
-
-    pair = packed_gram(block, snaps)
-    if cores > 1:
-        pair = exchange(pair_buf, core, cores, twin, pair_send, pair_recv, pair)
+        return totals[0][0], edges[0], totals[0][1]
+
+    parts = packed_gram(block, snaps)
     if strides:
         pl.semaphore_wait(relay_sem.at[len(strides) - 1], 2)
-    if chips > 1:
-        pair = exchange(chip_buf, mine, chips, chip, chip_send, chip_recv, pair)
-    high, low = pair
+    if len(sum_bufs) == 1:
+        everyone = lat_size * lon_size
+        parts = exchange(sum_bufs[0], lat * lon_size + lon, everyone, lambda at: at, 0, parts)
+    else:
+        parts = exchange(sum_bufs[0], lon, lon_size, lambda at: lat * lon_size + at, 0, parts)
+        parts = exchange(sum_bufs[1], lat, lat_size, lambda at: at * lon_size + lon, 1, parts)
+    local, edge, error = parts
+    ahead = place(snaps)
+    total, error = two_sum(local, error)
+    total = jnp.where(ahead > 0, total + error, total)
+    error = jnp.where(ahead > 0, 0.0, error)
 
     groups = snaps // SUBS
     sub = iota((SUBS, LANES), 0)
+    first, lower = factorize(
+        lambda g, k: total[:, g * snaps + k : g * snaps + k + 1], snaps
+    )
+    inverse = first[:, :snaps]
+    hold_ref[0] = first
+    gap = residual(total, error, edge, lower, snaps)
+    moved = pair_dot(gap, inverse, ((1,), (1,)))
+    moved = pair_dot(inverse, moved, ((1,), (0,)))
     start = []
     for g in range(groups):
-        unit = jnp.where(lane == sub + g * SUBS, 1.0, 0.0)
-        start.append(jnp.where(lane < snaps, unit, roll(high, snaps - g * snaps)))
-    first, lower = factorize(start, snaps)
-    inverse = first[:, :snaps]
-    solved = dot(inverse, block, ((1,), (0,)))
-    gap = residual(high, low, lower, snaps)
-    wide_inverse = jnp.concatenate([jnp.zeros_like(inverse), inverse], axis=0)
-    moved = pair_dot(gap, wide_inverse, ((1,), (1,)))
-    moved = pair_dot(
-        inverse, jnp.concatenate([moved, jnp.zeros_like(moved)], axis=1), ((1,), (0,))
-    )
-    start = []
-    for g in range(groups):
-        at = sub + g * SUBS
-        unit = jnp.where((lane == at) | (lane == at + snaps), 1.0, 0.0)
+        at = iota((SUBS, snaps), 0) + g * SUBS
+        unit = jnp.where(iota((SUBS, snaps), 1) == at, 1.0, 0.0)
         start.append(moved[g * SUBS : (g + 1) * SUBS] + unit)
-    second, _ = factorize(start, snaps)
-    modes = pair_dot(second[:, :snaps] * root, solved, ((1,), (0,)))
-    for f in range(2):
-        for i in range(cells):
-            at = (f * cells + i) * width
-            modes_ref[:, f, i, :] = modes[:, at : at + width]
-    factor_ref[...] = dot(second[:, : 2 * snaps], lower[:, : 2 * snaps], ((1,), (1,))) / root
+    hold_ref[1, :, :snaps] = moved
 
     for at, copy in enumerate(copies):
         if at == 0:
@@ -474,6 +480,57 @@
     for sent, send in pending:
         pltpu.make_async_copy(sent, sent, send).wait()
 
+    solved = dot(hold_ref[0][:, :snaps], block, ((1,), (0,)))
+    for at, part in enumerate(two(solved)):
+        solved_ref[at * snaps : (at + 1) * snaps, :] = part
+    second, lower_two = factorize(lambda g, k: start[g][:, k : k + 1], snaps)
+    turned = jnp.where(iota((snaps, LANES), 1) < snaps, second * root, 0.0)
+    bulk = turned.astype(jnp.bfloat16).astype(jnp.float32)
+    rest = turned - bulk
+    turn_ref[...] = bulk + pltpu.roll(bulk, snaps, 1) + pltpu.roll(rest, 2 * snaps, 1)
+    factor_ref[0] = lower
+    factor_ref[1] = lower_two
+
+
+def shifted(me, d, count):
+    if count & (count - 1) == 0:
+        return me ^ d
+    return (me + d) % count
+
+
+def peer_order(count):
+    return sorted(range(1, count), key=lambda d: (-((d >> 1) & 3), -(d >> 3), d))
+
+
+def finish(root, solved_ref, turn_ref, lower_ref, modes_hbm, factor_hbm, modes_ref, flat_ref, sem):
+    snaps, _, cells, width = modes_hbm.shape
+    left = turn_ref[...][:, : 3 * snaps].astype(jnp.bfloat16)
+    stores = []
+    for f in range(2):
+        for i in range(0, cells, 2):
+            at = (f * cells + i) * width
+            both = solved_ref[:, at : at + 2 * width]
+            right = jnp.concatenate([both, both[:snaps]], axis=0)
+            modes = lax.dot_general(
+                left, right, (((1,), (0,)), ((), ())), preferred_element_type=jnp.float32
+            )
+            for c in range(2):
+                modes_ref[f, i + c] = modes[:, c * width : (c + 1) * width]
+                stores.append(
+                    pltpu.make_async_copy(modes_ref.at[f, i + c], modes_hbm.at[:, f, i + c], sem)
+                )
+                stores[-1].start()
+    lower, lower_two = lower_ref[0], lower_ref[1]
+    shape = (snaps, LANES)
+    lower_two = pltpu.roll(lower_two, LANES - snaps, 1)
+    wide = jnp.concatenate([jnp.zeros((snaps, LANES), jnp.float32), lower_two], axis=0)
+    flat = dot(lower[:, : 2 * snaps], wide, ((1,), (0,))) / root
+    flat_ref[...] = jnp.transpose(flat)[:snaps, :snaps]
+    stores.append(pltpu.make_async_copy(flat_ref, factor_hbm, sem))
+    stores[-1].start()
+    for store in stores:
+        store.wait()
+
 
 def relay_strides(depth):
     strides, reach = [], 0
@@ -492,38 +549,59 @@
     vmem = pl.BlockSpec(memory_space=pltpu.VMEM)
     hbm = pl.BlockSpec(memory_space=pltpu.HBM)
     root = math.sqrt(2 * lat_size * cells * lon_size * width)
-    return pl.pallas_call(
+    if lat_size * lon_size <= DIRECT:
+        sum_bufs = [pltpu.VMEM((lat_size * lon_size, SUBS + 1, LANES), f32)]
+    else:
+        sum_bufs = [
+            pltpu.VMEM((lon_size, SUBS + 1, LANES), f32),
+            pltpu.VMEM((lat_size, 2 * SUBS + 1, LANES), f32),
+        ]
+    held = pl.pallas_call(
         functools.partial(kernel, sizes, root),
         out_shape=(
-            jax.ShapeDtypeStruct((snaps, 2, cells, width), f32),
-            jax.ShapeDtypeStruct((snaps, snaps), f32),
+            pltpu.VMEM((2 * snaps, 2 * cells * width), jnp.bfloat16),
+            pltpu.VMEM((snaps, LANES), f32),
+            pltpu.VMEM((2, snaps, LANES), f32),
         ),
         in_specs=[hbm, hbm],
-        out_specs=(vmem, vmem),
+        out_specs=(vmem, vmem, vmem),
         scratch_shapes=[
-            pltpu.VMEM((2, snaps, cells, width), f32),
+            pltpu.VMEM((2, cells, snaps, width), f32),
             pltpu.VMEM((2 * cells, snaps, width), f32),
-            pltpu.VMEM((2, 2, snaps, width), f32),
+            pltpu.VMEM((2, snaps, LANES), f32),
             pltpu.VMEM((2, 2, snaps, width), f32),
             pltpu.VMEM((SUBS, LANES), f32),
             pltpu.VMEM((2, SUBS, LANES), f32),
-            pltpu.VMEM((cores, 2, SUBS, LANES), f32),
-            pltpu.VMEM((chips, 2, SUBS, LANES), f32),
+            sum_bufs,
             dma((2,)),
             dma((2,)),
             dma((2,)),
             dma((2,)),
+            dma((len(sum_bufs),)),
+            dma((len(sum_bufs),)),
+            pltpu.SemaphoreType.REGULAR((max(len(relay_strides(lon_size // cores)), 1),)),
             dma,
-            dma,
-            dma,
-            dma,
-            pltpu.SemaphoreType.REGULAR((max(len(relay_strides(lon_size // cores)), 1),)),
-            dma((2,)),
         ],
         compiler_params=pltpu.CompilerParams(
             collective_id=0, has_side_effects=True, vmem_limit_bytes=VMEM_BYTES
         ),
     )(*(pltpu.with_memory_space_constraint(w, pltpu.HBM) for w in (wind_u, wind_v)))
+    anywhere = pl.BlockSpec(memory_space=pl.ANY)
+    return pl.pallas_call(
+        functools.partial(finish, root),
+        out_shape=(
+            jax.ShapeDtypeStruct((snaps, 2, cells, width), f32),
+            jax.ShapeDtypeStruct((snaps, snaps), f32),
+        ),
+        in_specs=[vmem, vmem, vmem],
+        out_specs=(anywhere, anywhere),
+        scratch_shapes=[
+            pltpu.VMEM((2, cells, snaps, width), f32),
+            pltpu.VMEM((snaps, snaps), f32),
+            dma,
+        ],
+        compiler_params=pltpu.CompilerParams(vmem_limit_bytes=VMEM_BYTES),
+    )(*held)
 
 
 def solution(mesh):

time: 20.5 us -> 19 us (0.927)
  local copies, waits for them, and re-layouts: 1.31 us -> 0 us
    unnamed x2 -> x0, local copies, waits for them, and re-layouts: 1.31 us -> none
    pallas_call x1 -> x2, Pallas kernels: 18.4 us -> 18.2 us  [the longest x1 17.2 us: shards(): pl.pallas_call(functools.partial(kernel, sizes, root), out_shape=(pltpu.V...]
where the time goes in v2:
time: 19 us; the launch traced here: 18.8 us
  Pallas kernels  18.2 us (96%)
  between operations  0.64 us (3%)
    pallas_call x1, Pallas kernels, shards(): pl.pallas_call(functools.partial(kernel, sizes, root), out_shape=(pltpu.V...  17.2 us
    pallas_call x1, Pallas kernels, shards(): pl.pallas_call(functools.partial(finish, root), out_shape=(jax.ShapeDtype...  0.93 us

profile of v2, /device:TPU:0, one launch (start us, length us, event | category | flops | bytes accessed | tf_op | source)
XLA Modules:
  0.0 18.8 jit_solution(14345838217888786186)
XLA Ops:
  0.6 17.2 %shard_map.41 = (bf16[64,2048]{1,0:T(8,128)(2,1)S(1)}, f32[32,128]{1,0:T(8,128)S(1)}, f32[2,32,128]{2,1,0:T(8,128)S(1)}) custom-call(f32[32,8,128]{2,1,0:T(8,128)} %u_hbm.1, f32[32,8,128]{2,1,0:T(8,128)} %v_hbm.1), custom_call_target="tpu_custom_call" | custom-call | tf_op jit(solution)/shard_map/pallas_call | solution.py:559
  17.9 0.9 %shard_map.42 = (f32[32,2,8,128]{3,2,1,0:T(8,128)}, f32[32,32]{1,0:T(8,128)}) custom-call(bf16[64,2048]{1,0:T(8,128)(2,1)S(1)} %get-tuple-element.5.solved_ref, f32[32,128]{1,0:T(8,128)S(1)} %get-tuple-element.6.turn_ref, f32[2,32,128]{2,1,0:T(8,128)S(1)} %get-tuple-element.7.lower_ref), custom_call_target="tpu_custom_call" | custom-call | tf_op jit(solution)/shard_map/pallas_call | solution.py:590

commit v3 on v2

--- a/solution.py
+++ b/solution.py
@@ -32,6 +32,12 @@
 def two(tile):
     high = tile.astype(jnp.bfloat16)
     return high, (tile - high.astype(jnp.float32)).astype(jnp.bfloat16)
+
+
+def three(tile):
+    high = tile.astype(jnp.bfloat16)
+    tile = tile - high.astype(jnp.float32)
+    return (high,) + two(tile)
 
 
 def pair_dot(left, right, dims):
@@ -75,29 +81,38 @@
     return out
 
 
-def factorize(source, n):
+def factorize(source, upper, n):
     groups = n // SUBS
     lane = iota((SUBS, LANES), 1)
     sub = iota((SUBS, LANES), 0)
-    columns = {
-        (g, k): spread(source(g, k)) for k in range(n) for g in range(k // SUBS, groups)
-    }
+    columns = {}
+
+    def bring(first, last, take):
+        for k in range(first * SUBS, min(last, groups) * SUBS):
+            for g in range(k // SUBS, groups):
+                columns[g, k] = spread(take(g, k))
+
+    bring(0, 2, source)
+    upper = list(upper)
     rows = [jnp.where(lane == sub + g * SUBS, 1.0, 0.0) for g in range(groups)]
     pivots = [None] * groups
     lower = [jnp.zeros((SUBS, LANES), jnp.float32)] * groups
     across = jnp.ones((SUBS, LANES), jnp.float32)
     for k in range(n):
         r, s = divmod(k, SUBS)
+        if s == 0 and r > 0:
+            bring(r + 1, r + 2, lambda g, j: upper[g][:, j : j + 1])
         pivot = spread(columns[r, k][s : s + 1, :])
         pivots[r] = pivot if s == 0 else jnp.where(sub == s, pivot, pivots[r])
         across = jnp.where(lane == n + k, pivot, across)
         inverse = 1.0 / pivot
         scaled = {g: columns[g, k] * inverse for g in range(r, groups)}
-        for j in range(k + 1, n):
+        for j in range(k + 1, min(n, (r + 2) * SUBS)):
             head = spread(columns[j // SUBS, k][j % SUBS : j % SUBS + 1, :])
             for g in range(j // SUBS, groups):
                 columns[g, j] = columns[g, j] - scaled[g] * head
         pivot_row = spread(rows[r][s : s + 1, :])
+        upper_row = jnp.broadcast_to(upper[r][s : s + 1, :], upper[r].shape)
         for g in range(r, groups):
             lower[g] = jnp.where(lane == n + k, columns[g, k], lower[g])
             factor = scaled[g]
@@ -106,6 +121,8 @@
                     continue
                 factor = jnp.where(sub > s, factor, 0.0)
             rows[g] = rows[g] - factor * pivot_row
+            if r + 2 < groups:
+                upper[g] = upper[g] - factor[:, : upper_row.shape[1]] * upper_row
     across = 1.0 / jnp.sqrt(across)
     out, left = [], []
     for g in range(groups):
@@ -115,13 +132,11 @@
     return jnp.concatenate(out, axis=0), jnp.concatenate(left, axis=0)
 
 
-def packed_gram(block, n):
+def gram_pair(tiles, n):
     groups = n // SUBS
-    peak = jnp.max(jnp.abs(block), axis=1, keepdims=True)
+    peak = jnp.max(functools.reduce(jnp.maximum, map(jnp.abs, tiles)), axis=1, keepdims=True)
     unit = power_above(jnp.broadcast_to(peak, (n, LANES)))
-    pieces = []
-    for at in range(0, block.shape[1], LANES):
-        pieces.append(fixed_slices(block[:, at : at + LANES], unit, (5, 12, 19)))
+    pieces = [fixed_slices(tile, unit, (5, 12, 19)) for tile in tiles]
     stack = jnp.concatenate(
         [jnp.concatenate([piece[a] for piece in pieces], axis=1) for a in range(4)], axis=0
     )
@@ -153,7 +168,10 @@
     rest = gather(far, 0) + (gather(far, 1) + gather(far, 2))
     high, low = two_sum(order[0], order[1])
     high, more = two_sum(high, order[2])
-    high, low = two_sum(high, (low + more) + (order[3] + rest))
+    return two_sum(high, (low + more) + (order[3] + rest))
+
+
+def message(high, low, n):
     ahead = place(n)
     edge = jnp.sum(jnp.where(ahead == 0, low, 0.0), axis=0, keepdims=True)
     return jnp.where(ahead > 0, low, high), edge
@@ -164,7 +182,7 @@
     return lane % n - (lane // n * SUBS + iota((SUBS, LANES), 0))
 
 
-def residual(total, error, edge, lower, n):
+def restore(total, error, edge, n):
     groups = n // SUBS
     shape = (n, n)
     row, col = iota(shape, 0), iota(shape, 1)
@@ -185,7 +203,11 @@
     diagonal = jnp.broadcast_to(diagonal[:, :n], shape)
     high = jnp.where(row >= col, whole, whole_flip)
     low = jnp.where(row > col, rest + whole_flip, rest_flip + whole)
-    low = jnp.where(row == col, rest + diagonal, low)
+    return high, jnp.where(row == col, rest + diagonal, low)
+
+
+def residual(high, low, lower, n):
+    row, col = iota((n, n), 0), iota((n, n), 1)
     peak = jnp.sqrt(jnp.sum(jnp.where(row == col, high, 0.0), axis=1, keepdims=True)) * 1.01
     unit = power_above(jnp.broadcast_to(peak, (n, LANES)))
     slices = fixed_slices(lower, unit, (8, 17, 26))
@@ -227,9 +249,12 @@
     wind_ref,
     x_ref,
     hold_ref,
+    ends_ref,
+    inner_ref,
     lat_in,
     lon_out,
     lon_in,
+    x_parts,
     sum_bufs,
     lat_send,
     lat_recv,
@@ -237,7 +262,8 @@
     lon_recv,
     sum_send,
     sum_recv,
-    relay_sem,
+    up_sem,
+    down_sem,
     local_sem,
 ):
     lat_size, lon_size, cores = sizes
@@ -254,6 +280,29 @@
     east = (lon + 1) % lon_size
     west = (lon + lon_size - 1) % lon_size
 
+    barrier = pltpu.get_barrier_semaphore()
+
+    first_z, last_z = z == 0, z == depth - 1
+    below, above = lon - cores, lon + cores
+    ring = [(lat, east), (lat, west)]
+    if cores == 2:
+        ring = [(lat, (lon + lon_size + 2 * core - 1) % lon_size)]
+    around = [
+        ((lat + a) % lat_size, z * cores + (core + b) % cores)
+        for a in range(lat_size)
+        for b in range(cores)
+        if a or b
+    ]
+
+    def greet(peer):
+        pl.semaphore_signal(barrier, inc=1, device_id=peer, device_id_type=MESH)
+
+    for peer in ring + around:
+        greet(peer)
+    pl.when(jnp.logical_not(first_z))(lambda: greet((lat, below)))
+    pl.when(jnp.logical_not(last_z))(lambda: greet((lat, above)))
+    callers = len(ring + around) + jnp.where(first_z, 0, 1) + jnp.where(last_z, 0, 1)
+
     loads = [
         pltpu.make_async_copy(hbm.at[:, i], wind_ref.at[f, i], local_sem)
         for f, hbm in enumerate((u_hbm, v_hbm))
@@ -262,22 +311,6 @@
     for load in loads:
         load.start()
 
-    barrier = pltpu.get_barrier_semaphore()
-
-    def along(d):
-        return [(lat, (z + depth + s) % depth * cores + core) for s in (d, -d)]
-
-    strides = relay_strides(depth)
-    peers = [
-        ((lat + a) % lat_size, z * cores + (core + b) % cores)
-        for a in range(lat_size)
-        for b in range(cores)
-        if a or b
-    ]
-    peers += [(lat, east), (lat, west)] + (along(1) if depth > 1 else [])
-    for peer in peers:
-        pl.semaphore_signal(barrier, inc=1, device_id=peer, device_id_type=MESH)
-
     pltpu.make_async_copy(wind_ref, wind_ref, local_sem).wait()
 
     lane = iota((SUBS, LANES), 1)
@@ -287,14 +320,14 @@
     for f in range(2):
         for i in range(cells):
             for t in range(parts):
-                q = (f * cells + i) * parts + t
+                q = (t * 2 + 1 - f) * cells + i
                 tile = winds[f][i][t * SUBS : (t + 1) * SUBS]
                 edges[t] = jnp.where(lane // 2 == q, roll(tile, 2 * q + 1), edges[t])
     while len(edges) > 1:
         edges = [sum(edges[at : at + 2]) for at in range(0, len(edges), 2)]
     lon_out[...] = edges[0]
 
-    pl.semaphore_wait(barrier, len(peers))
+    pl.semaphore_wait(barrier, callers)
 
     copies = []
     for way, target in ((0, lat_up), (1, lat_down)):
@@ -327,12 +360,21 @@
         else:
             copy.start()
 
-    def relay(at):
-        for peer in along(strides[at]):
-            pl.semaphore_signal(relay_sem.at[at], inc=1, device_id=peer, device_id_type=MESH)
-
-    if strides:
-        relay(0)
+    upper_core, lower_core = core == cores - 1, core == 0
+
+    def tell(sem, targets):
+        for target in targets:
+            pl.semaphore_signal(sem, inc=1, device_id=(lat, target), device_id_type=MESH)
+
+    def ascend():
+        tell(up_sem, [above, east] if cores > 1 else [above])
+
+    def descend():
+        tell(down_sem, [below, west] if cores > 1 else [below])
+
+    if depth > 1:
+        pl.when(jnp.logical_and(first_z, upper_core))(ascend)
+        pl.when(jnp.logical_and(last_z, lower_core))(descend)
 
     nlat = lat_size * cells
     step = 2.0 * math.pi / (lon_size * width)
@@ -358,13 +400,51 @@
         low = weight(i - 1) * winds[f][i - 1] if i > 0 else 0.0
         return high - low
 
-    for i in range(cells):
-        x_ref[i] = lon_inner(winds[1][i]) - lat_inner(0, i)
-        x_ref[cells + i] = lon_inner(winds[0][i]) + lat_inner(1, i)
-
-    for at in range(1, len(strides)):
-        pl.semaphore_wait(relay_sem.at[at - 1], 2)
-        relay(at)
+    def inner(f, i):
+        if f == 0:
+            return lon_inner(winds[1][i]) - lat_inner(0, i)
+        return lon_inner(winds[0][i]) + lat_inner(1, i)
+
+    sides = sorted({0, cells - 1})
+    middle = [i for i in range(cells) if i not in sides]
+    inside = (wide > 0) & (wide < LANES - 1)
+    rows_of = 2 * 2 * cells
+
+    def take_ends(tile, f, i, held):
+        at = f * cells + i
+        out = []
+        for t in range(parts):
+            moved = roll(tile[t * SUBS : (t + 1) * SUBS], 2 * at + 1)
+            out.append(held[t] + jnp.where(lane // 2 == at, moved, 0.0))
+        return out
+
+    held = [jnp.zeros((SUBS, LANES), jnp.float32)] * parts
+    tiles = []
+    for f in range(2):
+        for i in middle:
+            tile = inner(f, i) * scale(i)
+            x_ref[f * cells + i] = tile
+            held = take_ends(tile, f, i, held)
+            tiles.append(jnp.where(inside, tile, 0.0))
+        for i in sides:
+            x_ref[f * cells + i] = inner(f, i)
+    for t in range(parts):
+        ends_ref[t] = held[t]
+    if middle:
+        high, low = gram_pair(tiles, snaps)
+        inner_ref[0] = high
+        inner_ref[1] = low
+
+    if depth > 1:
+        @pl.when(jnp.logical_not(first_z))
+        def _():
+            pl.semaphore_wait(up_sem, 1)
+            pl.when(jnp.logical_and(upper_core, jnp.logical_not(last_z)))(ascend)
+
+        @pl.when(jnp.logical_not(last_z))
+        def _():
+            pl.semaphore_wait(down_sem, 1)
+            pl.when(jnp.logical_and(lower_core, jnp.logical_not(first_z)))(descend)
 
     for at, copy in enumerate(copies):
         if at == 0:
@@ -374,30 +454,41 @@
         else:
             copy.wait_recv()
 
-    ends = jnp.where(lane % 2 == 1, roll(lon_in[0], 1), roll(lon_in[1], LANES - 1))
-    sign = jnp.where(lane == LANES - 1, 1.0, jnp.where(lane == 0, -1.0, 0.0))
-
-    def lon_edge(f, i):
-        pieces = []
-        for t in range(parts):
-            q = (f * cells + i) * parts + t
-            pieces.append(sign * roll(ends, -(2 * q + 1)))
-        return jnp.concatenate(pieces, axis=0)
-
-    def lat_edge(f, i):
-        total = 0.0
-        if i == cells - 1:
-            total = total + weight(cells) * lat_in[1, f]
-        if i == 0:
-            total = total - weight(-1) * lat_in[0, f]
-        return total
-
-    columns = []
+    across = jnp.zeros((SUBS, LANES), jnp.float32)
     for i in range(cells):
-        columns.append((x_ref[i] + lon_edge(1, i) - lat_edge(0, i)) * scale(i))
-    for i in range(cells):
-        columns.append((x_ref[cells + i] + lon_edge(0, i) + lat_edge(1, i)) * scale(i))
-    block = jnp.concatenate(columns, axis=1)
+        across = jnp.where(lane // 2 % cells == i, scale(i), across)
+    across = jnp.where(lane < rows_of, across, 0.0)
+    ends = []
+    for t in range(parts):
+        from_east = roll(lon_in[1], -1 - t * rows_of)
+        from_west = roll(lon_in[0], 1 - t * rows_of)
+        ends.append(jnp.where(lane % 2 == 0, from_east, -from_west) * across)
+
+    held = [ends_ref[t] for t in range(parts)]
+    tiles = []
+    for f in range(2):
+        for i in sides:
+            edge = 0.0
+            if i == cells - 1:
+                edge = edge + weight(cells) * lat_in[1, f]
+            if i == 0:
+                edge = edge - weight(-1) * lat_in[0, f]
+            tile = x_ref[f * cells + i]
+            tile = (tile - edge if f == 0 else tile + edge) * scale(i)
+            x_ref[f * cells + i] = tile
+            held = take_ends(tile, f, i, held)
+            tiles.append(jnp.where(inside, tile, 0.0))
+    tiles.append(jnp.concatenate([held[t] + ends[t] for t in range(parts)], axis=0))
+    high, low = gram_pair(tiles, snaps)
+    if middle:
+        high, more = two_sum(high, inner_ref[0])
+        high, low = two_sum(high, low + (more + inner_ref[1]))
+
+    def whole_tile(f, i):
+        at = f * cells + i
+        tile = x_ref[at]
+        edge = jnp.concatenate([roll(ends[t], -2 * at - 1) for t in range(parts)], axis=0)
+        return jnp.where(inside, tile, tile + edge)
 
     pending = []
 
@@ -416,6 +507,12 @@
                 device_id_type=pl.DeviceIdType.LOGICAL,
             )
             copy.start()
+        if at == 0:
+            for f in range(2):
+                for i in range(cells):
+                    column = (f * cells + i) * width
+                    for index, part in enumerate(three(whole_tile(f, i))):
+                        x_parts[pl.ds(index * snaps, snaps), pl.ds(column, width)] = part
         arrived = buf.at[pl.ds(0, count - 1)]
         pending.append((arrived, sum_send.at[at]))
         pltpu.make_async_copy(arrived, arrived, sum_recv.at[at]).wait()
@@ -438,16 +535,14 @@
             totals = merged
         return totals[0][0], edges[0], totals[0][1]
 
-    parts = packed_gram(block, snaps)
-    if strides:
-        pl.semaphore_wait(relay_sem.at[len(strides) - 1], 2)
+    bundle = message(high, low, snaps)
     if len(sum_bufs) == 1:
         everyone = lat_size * lon_size
-        parts = exchange(sum_bufs[0], lat * lon_size + lon, everyone, lambda at: at, 0, parts)
+        bundle = exchange(sum_bufs[0], lat * lon_size + lon, everyone, lambda at: at, 0, bundle)
     else:
-        parts = exchange(sum_bufs[0], lon, lon_size, lambda at: lat * lon_size + at, 0, parts)
-        parts = exchange(sum_bufs[1], lat, lat_size, lambda at: at * lon_size + lon, 1, parts)
-    local, edge, error = parts
+        bundle = exchange(sum_bufs[0], lon, lon_size, lambda at: lat * lon_size + at, 0, bundle)
+        bundle = exchange(sum_bufs[1], lat, lat_size, lambda at: at * lon_size + lon, 1, bundle)
+    local, edge, error = bundle
     ahead = place(snaps)
     total, error = two_sum(local, error)
     total = jnp.where(ahead > 0, total + error, total)
@@ -455,12 +550,15 @@
 
     groups = snaps // SUBS
     sub = iota((SUBS, LANES), 0)
+    high, low = restore(total, error, edge, snaps)
     first, lower = factorize(
-        lambda g, k: total[:, g * snaps + k : g * snaps + k + 1], snaps
+        lambda g, k: total[:, g * snaps + k : g * snaps + k + 1],
+        [high[g * SUBS : (g + 1) * SUBS] for g in range(groups)],
+        snaps,
     )
     inverse = first[:, :snaps]
     hold_ref[0] = first
-    gap = residual(total, error, edge, lower, snaps)
+    gap = residual(high, low, lower, snaps)
     moved = pair_dot(gap, inverse, ((1,), (1,)))
     moved = pair_dot(inverse, moved, ((1,), (0,)))
     start = []
@@ -480,14 +578,25 @@
     for sent, send in pending:
         pltpu.make_async_copy(sent, sent, send).wait()
 
-    solved = dot(hold_ref[0][:, :snaps], block, ((1,), (0,)))
-    for at, part in enumerate(two(solved)):
-        solved_ref[at * snaps : (at + 1) * snaps, :] = part
-    second, lower_two = factorize(lambda g, k: start[g][:, k : k + 1], snaps)
-    turned = jnp.where(iota((snaps, LANES), 1) < snaps, second * root, 0.0)
-    bulk = turned.astype(jnp.bfloat16).astype(jnp.float32)
-    rest = turned - bulk
-    turn_ref[...] = bulk + pltpu.roll(bulk, snaps, 1) + pltpu.roll(rest, 2 * snaps, 1)
+    w = [part.astype(jnp.float32) for part in three(hold_ref[0])]
+    quarters = LANES // snaps
+    terms = [(0, 0), (0, 1), (0, 2), (1, 0), (1, 1), (2, 0)]
+    left = []
+    for at in range(0, len(terms), quarters):
+        tiles = [
+            pltpu.roll(w[a], index * snaps, 1) if index else w[a]
+            for index, (a, b) in enumerate(terms[at : at + quarters])
+        ]
+        left.append(sum(tiles[1:], tiles[0]).astype(jnp.bfloat16))
+    left = jnp.concatenate(left, axis=1)[:, : len(terms) * snaps]
+    for at in range(0, 2 * cells * width, 2 * width):
+        x = [x_parts[b * snaps : (b + 1) * snaps, at : at + 2 * width] for b in range(3)]
+        right = jnp.concatenate([x[b] for a, b in terms], axis=0)
+        solved_ref[:, at : at + 2 * width] = lax.dot_general(
+            left, right, (((1,), (0,)), ((), ())), preferred_element_type=jnp.float32
+        )
+    second, lower_two = factorize(lambda g, k: start[g][:, k : k + 1], start, snaps)
+    turn_ref[...] = second * root
     factor_ref[0] = lower
     factor_ref[1] = lower_two
 
@@ -504,16 +613,19 @@
 
 def finish(root, solved_ref, turn_ref, lower_ref, modes_hbm, factor_hbm, modes_ref, flat_ref, sem):
     snaps, _, cells, width = modes_hbm.shape
-    left = turn_ref[...][:, : 3 * snaps].astype(jnp.bfloat16)
+    bulk, rest = two(turn_ref[...][:, :snaps])
     stores = []
+
+    def one(m, n):
+        return lax.dot_general(
+            m, n, (((1,), (0,)), ((), ())), preferred_element_type=jnp.float32
+        )
+
     for f in range(2):
         for i in range(0, cells, 2):
             at = (f * cells + i) * width
-            both = solved_ref[:, at : at + 2 * width]
-            right = jnp.concatenate([both, both[:snaps]], axis=0)
-            modes = lax.dot_general(
-                left, right, (((1,), (0,)), ((), ())), preferred_element_type=jnp.float32
-            )
+            main, tail = two(solved_ref[:, at : at + 2 * width])
+            modes = one(bulk, main) + (one(bulk, tail) + one(rest, main))
             for c in range(2):
                 modes_ref[f, i + c] = modes[:, c * width : (c + 1) * width]
                 stores.append(
@@ -530,14 +642,6 @@
     stores[-1].start()
     for store in stores:
         store.wait()
-
-
-def relay_strides(depth):
-    strides, reach = [], 0
-    while reach < depth // 2:
-        strides.append(max(reach, 1))
-        reach += strides[-1]
-    return strides
 
 
 def shards(sizes, wind_u, wind_v):
@@ -559,7 +663,7 @@
     held = pl.pallas_call(
         functools.partial(kernel, sizes, root),
         out_shape=(
-            pltpu.VMEM((2 * snaps, 2 * cells * width), jnp.bfloat16),
+            pltpu.VMEM((snaps, 2 * cells * width), f32),
             pltpu.VMEM((snaps, LANES), f32),
             pltpu.VMEM((2, snaps, LANES), f32),
         ),
@@ -569,9 +673,12 @@
             pltpu.VMEM((2, cells, snaps, width), f32),
             pltpu.VMEM((2 * cells, snaps, width), f32),
             pltpu.VMEM((2, snaps, LANES), f32),
+            pltpu.VMEM((snaps // SUBS, SUBS, LANES), f32),
+            pltpu.VMEM((2, SUBS, LANES), f32),
             pltpu.VMEM((2, 2, snaps, width), f32),
             pltpu.VMEM((SUBS, LANES), f32),
             pltpu.VMEM((2, SUBS, LANES), f32),
+            pltpu.VMEM((3 * snaps, 2 * cells * width), jnp.bfloat16),
             sum_bufs,
             dma((2,)),
             dma((2,)),
@@ -579,7 +686,8 @@
             dma((2,)),
             dma((len(sum_bufs),)),
             dma((len(sum_bufs),)),
-            pltpu.SemaphoreType.REGULAR((max(len(relay_strides(lon_size // cores)), 1),)),
+            pltpu.SemaphoreType.REGULAR,
+            pltpu.SemaphoreType.REGULAR,
             dma,
         ],
         compiler_params=pltpu.CompilerParams(

time: 19 us -> 17.8 us (0.937)
  Pallas kernels: 18.2 us -> 17 us
    pallas_call x1, Pallas kernels: 17.2 us -> 16 us  [shards(): pl.pallas_call(functools.partial(kernel, sizes, root), out_shape=(pltpu.V...]
where the time goes in v3:
time: 17.8 us; the launch traced here: 17.6 us
  Pallas kernels  17 us (96%)
  between operations  0.64 us (4%)
    pallas_call x1, Pallas kernels, shards(): pl.pallas_call(functools.partial(kernel, sizes, root), out_shape=(pltpu.V...  16 us
    pallas_call x1, Pallas kernels, shards(): pl.pallas_call(functools.partial(finish, root), out_shape=(jax.ShapeDtype...  0.95 us

profile of v3, /device:TPU:0, one launch (start us, length us, event | category | flops | bytes accessed | tf_op | source)
XLA Modules:
  0.0 17.6 jit_solution(12194372317895526117)
XLA Ops:
  0.6 16.0 %shard_map.41 = (f32[32,2048]{1,0:T(8,128)S(1)}, f32[32,128]{1,0:T(8,128)S(1)}, f32[2,32,128]{2,1,0:T(8,128)S(1)}) custom-call(f32[32,8,128]{2,1,0:T(8,128)} %u_hbm.1, f32[32,8,128]{2,1,0:T(8,128)} %v_hbm.1), custom_call_target="tpu_custom_call" | custom-call | tf_op jit(solution)/shard_map/pallas_call | solution.py:663
  16.7 1.0 %shard_map.42 = (f32[32,2,8,128]{3,2,1,0:T(8,128)}, f32[32,32]{1,0:T(8,128)}) custom-call(f32[32,2048]{1,0:T(8,128)S(1)} %get-tuple-element.5.solved_ref, f32[32,128]{1,0:T(8,128)S(1)} %get-tuple-element.6.turn_ref, f32[2,32,128]{2,1,0:T(8,128)S(1)} %get-tuple-element.7.lower_ref), custom_call_target="tpu_custom_call" | custom-call | tf_op jit(solution)/shard_map/pallas_call | solution.py:698

commit v4 on v3

--- a/solution.py
+++ b/solution.py
@@ -145,30 +145,21 @@
     )
     quarter = iota((SUBS, LANES), 1) // n
 
-    def tile(a, g):
-        at = a * n + g * SUBS
-        return roll(gram[at : at + SUBS], a * n)
-
-    near, far = [], []
-    for g in range(groups):
-        turned = [tile(a, g) for a in range(4)]
-        held = [turned[0]] + [jnp.where(quarter >= a, turned[a], 0.0) for a in range(1, 4)]
-        past = [jnp.where(quarter < a, turned[a], 0.0) for a in range(1, 4)]
-        near.append((held[0] + held[3]) + (held[1] + held[2]))
-        far.append((past[0] + past[2]) + past[1])
-
-    def gather(tiles, order):
+    def part(a, b):
         total = None
         for g in range(groups):
-            moved = roll(tiles[g], n * (g - order))
+            at = a * n + g * SUBS
+            moved = roll(gram[at : at + SUBS], n * (g - b))
             total = moved if total is None else jnp.where(quarter == g, moved, total)
         return total
 
-    order = [gather(near, o) for o in range(4)]
-    rest = gather(far, 0) + (gather(far, 1) + gather(far, 2))
-    high, low = two_sum(order[0], order[1])
-    high, more = two_sum(high, order[2])
-    return two_sum(high, (low + more) + (order[3] + rest))
+    def term(a, b):
+        return part(a, b) if a == b else part(a, b) + part(b, a)
+
+    high, low = two_sum(term(0, 0), term(0, 1))
+    high, more = two_sum(high, term(0, 2) + term(1, 1))
+    tiny = (term(1, 3) + term(2, 2)) + (term(2, 3) + term(3, 3))
+    return two_sum(high, (low + more) + ((term(0, 3) + term(1, 2)) + tiny))
 
 
 def message(high, low, n):
@@ -352,13 +343,10 @@
                 device_id_type=MESH,
             )
         )
-    for at, copy in enumerate(copies):
-        if at == 0:
-            pl.when(lat < lat_size - 1)(copy.start)
-        elif at == 1:
-            pl.when(lat > 0)(copy.start)
-        else:
-            copy.start()
+    for copy in copies[2:]:
+        copy.start()
+    pl.when(lat < lat_size - 1)(copies[0].start)
+    pl.when(lat > 0)(copies[1].start)
 
     upper_core, lower_core = core == cores - 1, core == 0
 

time: 17.8 us -> 17.7 us (level)
  no operation moved by 1% of the time
where the time goes in v4:
time: 17.7 us; the launch traced here: 17.6 us
  Pallas kernels  16.9 us (95%)
  between operations  0.64 us (4%)
    pallas_call x1, Pallas kernels, shards(): pl.pallas_call(functools.partial(kernel, sizes, root), out_shape=(pltpu.V...  16 us
    pallas_call x1, Pallas kernels, shards(): pl.pallas_call(functools.partial(finish, root), out_shape=(jax.ShapeDtype...  0.95 us

profile of v4, /device:TPU:0, one launch (start us, length us, event | category | flops | bytes accessed | tf_op | source)
XLA Modules:
  0.0 17.6 jit_solution(17196764888138035086)
XLA Ops:
  0.6 16.0 %shard_map.41 = (f32[32,2048]{1,0:T(8,128)S(1)}, f32[32,128]{1,0:T(8,128)S(1)}, f32[2,32,128]{2,1,0:T(8,128)S(1)}) custom-call(f32[32,8,128]{2,1,0:T(8,128)} %u_hbm.1, f32[32,8,128]{2,1,0:T(8,128)} %v_hbm.1), custom_call_target="tpu_custom_call" | custom-call | tf_op jit(solution)/shard_map/pallas_call | solution.py:651
  16.6 1.0 %shard_map.42 = (f32[32,2,8,128]{3,2,1,0:T(8,128)}, f32[32,32]{1,0:T(8,128)}) custom-call(f32[32,2048]{1,0:T(8,128)S(1)} %get-tuple-element.5.solved_ref, f32[32,128]{1,0:T(8,128)S(1)} %get-tuple-element.6.turn_ref, f32[2,32,128]{2,1,0:T(8,128)S(1)} %get-tuple-element.7.lower_ref), custom_call_target="tpu_custom_call" | custom-call | tf_op jit(solution)/shard_map/pallas_call | solution.py:686

commit v5 on v4

--- a/solution.py
+++ b/solution.py
@@ -81,7 +81,7 @@
     return out
 
 
-def factorize(source, upper, n):
+def factorize(source, upper, n, base):
     groups = n // SUBS
     lane = iota((SUBS, LANES), 1)
     sub = iota((SUBS, LANES), 0)
@@ -104,7 +104,7 @@
             bring(r + 1, r + 2, lambda g, j: upper[g][:, j : j + 1])
         pivot = spread(columns[r, k][s : s + 1, :])
         pivots[r] = pivot if s == 0 else jnp.where(sub == s, pivot, pivots[r])
-        across = jnp.where(lane == n + k, pivot, across)
+        across = jnp.where(lane == base + k, pivot, across)
         inverse = 1.0 / pivot
         scaled = {g: columns[g, k] * inverse for g in range(r, groups)}
         for j in range(k + 1, min(n, (r + 2) * SUBS)):
@@ -114,7 +114,7 @@
         pivot_row = spread(rows[r][s : s + 1, :])
         upper_row = jnp.broadcast_to(upper[r][s : s + 1, :], upper[r].shape)
         for g in range(r, groups):
-            lower[g] = jnp.where(lane == n + k, columns[g, k], lower[g])
+            lower[g] = jnp.where(lane == base + k, columns[g, k], lower[g])
             factor = scaled[g]
             if g == r:
                 if s == SUBS - 1:
@@ -127,7 +127,7 @@
     out, left = [], []
     for g in range(groups):
         out.append(rows[g] * (1.0 / jnp.sqrt(pivots[g])))
-        keep = (lane >= n) & (lane - n - g * SUBS <= sub)
+        keep = (lane >= base) & (lane - base - g * SUBS <= sub)
         left.append(jnp.where(keep, lower[g] * across, 0.0))
     return jnp.concatenate(out, axis=0), jnp.concatenate(left, axis=0)
 
@@ -543,6 +543,7 @@
         lambda g, k: total[:, g * snaps + k : g * snaps + k + 1],
         [high[g * SUBS : (g + 1) * SUBS] for g in range(groups)],
         snaps,
+        snaps,
     )
     inverse = first[:, :snaps]
     hold_ref[0] = first
@@ -583,7 +584,7 @@
         solved_ref[:, at : at + 2 * width] = lax.dot_general(
             left, right, (((1,), (0,)), ((), ())), preferred_element_type=jnp.float32
         )
-    second, lower_two = factorize(lambda g, k: start[g][:, k : k + 1], start, snaps)
+    second, lower_two = factorize(lambda g, k: start[g][:, k : k + 1], start, snaps, 0)
     turn_ref[...] = second * root
     factor_ref[0] = lower
     factor_ref[1] = lower_two
@@ -602,6 +603,11 @@
 def finish(root, solved_ref, turn_ref, lower_ref, modes_hbm, factor_hbm, modes_ref, flat_ref, sem):
     snaps, _, cells, width = modes_hbm.shape
     bulk, rest = two(turn_ref[...][:, :snaps])
+    lower, lower_two = lower_ref[0][:, : 2 * snaps], lower_ref[1][:, :snaps]
+    wide = jnp.concatenate([jnp.zeros_like(lower_two), lower_two], axis=0)
+    wide = jnp.concatenate([wide, jnp.zeros((2 * snaps, LANES - snaps), jnp.float32)], axis=1)
+    flat = dot(lower, wide, ((1,), (0,))) / root
+    flat = jnp.transpose(flat)[:snaps, :snaps]
     stores = []
 
     def one(m, n):
@@ -620,12 +626,7 @@
                     pltpu.make_async_copy(modes_ref.at[f, i + c], modes_hbm.at[:, f, i + c], sem)
                 )
                 stores[-1].start()
-    lower, lower_two = lower_ref[0], lower_ref[1]
-    shape = (snaps, LANES)
-    lower_two = pltpu.roll(lower_two, LANES - snaps, 1)
-    wide = jnp.concatenate([jnp.zeros((snaps, LANES), jnp.float32), lower_two], axis=0)
-    flat = dot(lower[:, : 2 * snaps], wide, ((1,), (0,))) / root
-    flat_ref[...] = jnp.transpose(flat)[:snaps, :snaps]
+    flat_ref[...] = flat
     stores.append(pltpu.make_async_copy(flat_ref, factor_hbm, sem))
     stores[-1].start()
     for store in stores:

time: 17.7 us -> 17.7 us (level)
  no operation moved by 1% of the time
where the time goes in v5:
time: 17.7 us; the launch traced here: 17.5 us
  Pallas kernels  16.9 us (95%)
  between operations  0.64 us (4%)
    pallas_call x1, Pallas kernels, shards(): pl.pallas_call(functools.partial(kernel, sizes, root), out_shape=(pltpu.V...  16 us
    pallas_call x1, Pallas kernels, shards(): pl.pallas_call(functools.partial(finish, root), out_shape=(jax.ShapeDtype...  0.91 us

profile of v5, /device:TPU:0, one launch (start us, length us, event | category | flops | bytes accessed | tf_op | source)
XLA Modules:
  0.0 17.5 jit_solution(5309449783734612909)
XLA Ops:
  0.6 16.0 %shard_map.41 = (f32[32,2048]{1,0:T(8,128)S(1)}, f32[32,128]{1,0:T(8,128)S(1)}, f32[2,32,128]{2,1,0:T(8,128)S(1)}) custom-call(f32[32,8,128]{2,1,0:T(8,128)} %u_hbm.1, f32[32,8,128]{2,1,0:T(8,128)} %v_hbm.1), custom_call_target="tpu_custom_call" | custom-call | tf_op jit(solution)/shard_map/pallas_call | solution.py:652
  16.6 0.9 %shard_map.42 = (f32[32,2,8,128]{3,2,1,0:T(8,128)}, f32[32,32]{1,0:T(8,128)}) custom-call(f32[32,2048]{1,0:T(8,128)S(1)} %get-tuple-element.5.solved_ref, f32[32,128]{1,0:T(8,128)S(1)} %get-tuple-element.6.turn_ref, f32[2,32,128]{2,1,0:T(8,128)S(1)} %get-tuple-element.7.lower_ref), custom_call_target="tpu_custom_call" | custom-call | tf_op jit(solution)/shard_map/pallas_call | solution.py:687
